TPU v7x, 32 devices: a whole 2x2x4 slice. The times are simulated.
32 devices in a mesh: lon: 16 (over z, x, core), lat: 2 (over y).
Axes of the slice: x: 2, y: 2, z: 4, core: 2. Of those that a mesh axis runs over, the one named last changes fastest.
Arguments:
- fields: bfloat16 [64, 1792, 256], P('lat', 'lon'), may hold values from -6 to 6
- cotangent: bfloat16 [64, 1792, 256], P('lat', 'lon'), may hold values from -6 to 6
- kernel: float32 [31, 256], replicated, may hold values from -1 to 1
- up_weight: bfloat16 [256, 1024], replicated, may hold values from -0.375 to 0.375
- down_weight: bfloat16 [1024, 256], replicated, may hold values from -0.1875 to 0.1875
Outputs:
- output: bfloat16 [64, 1792, 256], P('lat', 'lon')
- field_grad: bfloat16 [64, 1792, 256], P('lat', 'lon')
- kernel_grad: float32 [31, 256], replicated
- up_grad: float32 [256, 1024], replicated
- down_grad: float32 [1024, 256], replicated
All inputs are finite; a program needn't handle non-finite values.
Results may differ from a plain program's by a relative error of at most 0.0055.
Values may be sent and summed in bfloat16 or wider, within the bound.
No kernel may reach another device: no remote copies, remote signals or barrier semaphores. Data moves between devices by JAX's collectives and lax.ppermute only.
A program may use at most 128 MiB of HBM per device.

v0:
```python
import math
import jax
import jax.numpy as jnp
from jax import lax
from jax.sharding import PartitionSpec as P

KERNEL_SPACING = 4


def passed_along(value, axis, by):
    count = lax.axis_size(axis)
    return lax.ppermute(value, axis, [(i, (i + by) % count) for i in range(count)])


def gelu_tanh(values):
    return jax.nn.gelu(values, approximate=True)


def per_device(fields, cotangent, kernel, up_weight, down_weight):
    rows, column_list, channels = fields.shape
    taps = kernel.shape[0]
    taps_half_span = taps // 2
    border_extent = KERNEL_SPACING * taps_half_span
    blocks_out = -(-border_extent // column_list)
    sides = []
    for direction in (1, -1):
        current = fields
        current = passed_along(current, "lon", direction)
        passed = [current]
        sides.append(passed)
    whole = jnp.concatenate(sides[0][::-1] + [fields] + sides[1], axis=1)
    first = blocks_out * column_list - border_extent
    wrapped_input = whole[:, first : first + column_list + 2 * border_extent]
    conv = jnp.zeros((rows, column_list, channels), jnp.float32)
    for index_of_tap in range(taps):
        tap_window = wrapped_input[
            :, KERNEL_SPACING * index_of_tap : KERNEL_SPACING * index_of_tap + column_list
        ].astype(jnp.float32)
        conv = conv + kernel[index_of_tap] * tap_window
    conv = conv.reshape(rows * column_list, channels)
    center = jnp.mean(conv, axis=-1, keepdims=True)
    deviation = conv - center
    spread = jnp.mean(deviation * deviation, axis=-1, keepdims=True)
    inv_scale = lax.rsqrt(spread + 1e-06)
    normed = deviation * inv_scale
    normed_low = normed.astype(jnp.bfloat16)
    hidden = jnp.dot(normed_low, up_weight, preferred_element_type=jnp.float32)
    activated, pullback = jax.vjp(gelu_tanh, hidden)
    activated_low = activated.astype(jnp.bfloat16)
    flat_in = fields.reshape(rows * column_list, channels)
    flat_cot = cotangent.reshape(rows * column_list, channels)
    output = (
        flat_in.astype(jnp.float32)
        + jnp.dot(activated_low, down_weight, preferred_element_type=jnp.float32)
    ).astype(jnp.bfloat16)
    output = output.reshape(rows, column_list, channels)
    contract_last = (((1,), (1,)), ((), ()))
    contract_first = (((0,), (0,)), ((), ()))
    upstream = lax.dot_general(
        flat_cot, down_weight, contract_last, preferred_element_type=jnp.float32
    )
    hidden_grad = pullback(upstream)[0].astype(jnp.bfloat16)
    normed_grad = lax.dot_general(
        hidden_grad, up_weight, contract_last, preferred_element_type=jnp.float32
    )
    mean_grad = jnp.mean(normed_grad, axis=-1, keepdims=True)
    mean_cross = jnp.mean(normed_grad * normed, axis=-1, keepdims=True)
    conv_grad = (inv_scale * (normed_grad - mean_grad - normed * mean_cross)).reshape(
        rows, column_list, channels
    )
    layout = [(1, max(0, column_list - border_extent), column_list)]
    layout = layout + [(-1, 0, min(column_list, column_list + border_extent - column_list))]
    pieces = [
        passed_along(conv_grad[:, lower:upper].astype(jnp.bfloat16), "lon", moved).astype(
            jnp.float32
        )
        for moved, lower, upper in layout
    ]
    grad_padded = jnp.concatenate(pieces[:blocks_out] + [conv_grad] + pieces[blocks_out:], axis=1)
    conv_back = jnp.zeros((rows, column_list, channels), jnp.float32)
    for index_of_tap in range(taps):
        window_start = KERNEL_SPACING * (2 * taps_half_span - index_of_tap)
        conv_back = (
            conv_back
            + kernel[index_of_tap] * grad_padded[:, window_start : window_start + column_list]
        )
    field_grad = (cotangent.astype(jnp.float32) + conv_back).astype(jnp.bfloat16)
    kernel_terms = jnp.stack(
        [
            jnp.sum(
                wrapped_input[
                    :, KERNEL_SPACING * index_of_tap : KERNEL_SPACING * index_of_tap + column_list
                ].astype(jnp.float32)
                * conv_grad,
                axis=(0, 1),
            )
            for index_of_tap in range(taps)
        ]
    )
    grad_up = lax.dot_general(
        normed_low, hidden_grad, contract_first, preferred_element_type=jnp.float32
    )
    grad_down = lax.dot_general(
        activated_low, flat_cot, contract_first, preferred_element_type=jnp.float32
    )
    summed = lax.psum((kernel_terms, grad_up, grad_down), ("lon", "lat"))
    factor = 1.0 / math.sqrt(rows * column_list * lax.axis_size("lon") * lax.axis_size("lat"))
    return (output, field_grad, summed[0] * factor, summed[1] * factor, summed[2] * factor)


def solution(mesh):
    placed = (P("lat", "lon", None), P("lat", "lon", None), P(), P(), P())
    return jax.shard_map(
        per_device,
        mesh=mesh,
        in_specs=placed,
        out_specs=(P("lat", "lon", None), P("lat", "lon", None), P(), P(), P()),
        check_vma=False,
    )
```

profile of v0, /device:TPU:0, one launch (start us, length us, event | category | flops | bytes accessed | tf_op | source)
XLA Modules:
  0.0 282.3 jit_solution(12317122125374097740)
XLA Ops:
  7.7 5.0 %collective-permute-start.1 = (bf16[32,112,256]{2,1,0:T(8,128)(2,1)}, bf16[32,112,256]{2,1,0:T(8,128)(2,1)S(1)}, u32[]{:S(2)}, u32[]{:S(2)}) collective-permute-start(bf16[32,112,256]{2,1,0:T(8,128)(2,1)} %param.5), channel_id=1, source_target_pairs={{0,30},{2,0},{4,2},{6,4},{8,6},{10,8},{12,10},{14,12},{16,14},{18,... | collective-permute-start | bytes 5505032 | tf_op jit(solution)/shard_map/ppermute | solution.py:12
  14.8 19.2 %collective-permute-done = bf16[32,112,256]{2,1,0:T(8,128)(2,1)S(1)} collective-permute-done((bf16[32,112,256]{2,1,0:T(8,128)(2,1)}, bf16[32,112,256]{2,1,0:T(8,128)(2,1)S(1)}, u32[]{:S(2)}, u32[]{:S(2)}) %collective-permute-start) | collective-permute-done | bytes 1835040 | tf_op jit(solution)/shard_map/ppermute | solution.py:12
  34.8 16.6 %fusion.161 = (f32[32,112]{1,0:T(8,128)S(1)}, f32[32,112,256]{2,1,0:T(8,128)}) fusion(bf16[32,224,256]{2,1,0:T(8,128)(2,1)S(1)} %constant_dynamic-update-slice_fusion.2, f32[256]{0:T(256)S(1)} %bitcast.116, f32[256]{0:T(256)S(1)} %bitcast.118, f32[256]{0:T(256)S(1)} %bitcast.122, f32[256]{0:T(256)S(1)} %bitcast.124, f32[256]{0:T(256)S(1)} %bitcast.126, ...), kind=kLoop, calls=%fused_computation.300 | loop fusion | flops 85324288 | bytes 60601344 | tf_op jit(solution)/shard_map/reduce_sum | solution.py:41
  51.4 2.7 multiply_reduce_fusion.2
  54.3 3.4 %fusion.159 = bf16[3584,256]{1,0:T(8,128)(2,1)S(1)} fusion(f32[32,112,256]{2,1,0:T(8,128)} %get-tuple-element.41, f32[3584]{0:T(1024)S(1)} %rsqrt.12, f32[3584]{0:T(1024)S(1)} %div.15), kind=kLoop, calls=%fused_computation.287 | loop fusion | flops 2752512 | bytes 5533696 | tf_op jit(solution)/shard_map/convert_element_type | solution.py:46
  57.7 7.9 %multiply_convert_fusion = (bf16[3584,1024]{1,0:T(8,128)(2,1)S(1)}, f32[3584,1024]{1,0:T(8,128)}) fusion(bf16[3584,256]{1,0:T(8,128)(2,1)S(1)} %fusion.159, bf16[256,1024]{1,0:T(8,128)(2,1)S(1)} %copy-done), kind=kOutput, calls=%fused_computation.65 | convolution fusion | flops 1912078336 | bytes 24379392 | tf_op jit(solution)/shard_map/dot_general | solution.py:47
  65.6 15.9 %fusion.6 = bf16[3584,1024]{1,0:T(8,128)(2,1)S(1)} fusion(f32[3584,1024]{1,0:T(8,128)} %get-tuple-element.78, bf16[3584,256]{1,0:T(8,128)(2,1)} %bitcast.94, bf16[1024,256]{1,0:T(8,128)(2,1)S(1)} %copy-done.11), kind=kOutput, calls=%fused_computation.64 | convolution fusion | flops 1952448512 | bytes 24379392 | tf_op jit(solution)/shard_map/dot_general | solution.py:59
  81.5 2.5 fusion.160
  84.0 2.7 subtract_multiply_fusion
  86.7 9.4 %fusion.47 = (f32[256]{0:T(256)}, f32[256]{0:T(256)}, f32[256]{0:T(256)}, f32[256]{0:T(256)}, f32[256]{0:T(256)}, /*index=5*/f32[256]{0:T(256)}, f32[256]{0:T(25...) fusion(f32[32,112,256]{2,1,0:T(8,128)S(1)} %bitcast.89, ...), kind=kLoop, calls=%fused_computation.167 | loop fusion | flops 41283840 | bytes 31210496 | tf_op jit(solution)/shard_map/reduce_sum | solution.py:90
  96.1 9.5 %fusion.67 = (f32[256]{0:T(256)S(1)}, f32[256]{0:T(256)S(1)}, f32[256]{0:T(256)S(1)}, f32[256]{0:T(256)S(1)}, f32[256]{0:T(256)S(1)}, /*index=5*/f32[256]{0:T(25...) fusion(f32[32,112,256]{2,1,0:T(8,128)S(1)} %bitcast.90, ...), kind=kLoop, calls=%fused_computation.187 | loop fusion | flops 44036096 | bytes 33046528 | tf_op jit(solution)/shard_map/reduce_sum | solution.py:90
  105.7 2.0 copy.14
  107.6 3.1 %fusion.167 = f32[1024,256]{1,0:T(8,128)} fusion(bf16[3584,1024]{1,0:T(8,128)(2,1)S(1)} %get-tuple-element.77, bf16[3584,256]{1,0:T(8,128)(2,1)S(1)} %bitcast.95), kind=kOutput, calls=%fused_computation.305 | convolution fusion | flops 1879048192 | bytes 10223616 | tf_op jit(solution)/shard_map/dot_general | solution.py:103
  112.2 3.9 %collective-permute-start.2 = (bf16[32,60,256]{2,0,1:T(8,128)(2,1)}, bf16[32,60,256]{2,0,1:T(8,128)(2,1)S(1)}, u32[]{:S(2)}, u32[]{:S(2)}) collective-permute-start(bf16[32,60,256]{2,0,1:T(8,128)(2,1)} %get-tuple-element.42), channel_id=1, source_target_pairs={{0,30},{2,0},{4,2},{6,4},{8,6},{10,8},{12,10},{14,12},{16,14},{18,... | collective-permute-start | bytes 2949128 | tf_op jit(solution)/shard_map/ppermute | solution.py:12
  116.1 14.4 %collective-permute-start.3 = (bf16[32,60,256]{2,0,1:T(8,128)(2,1)}, bf16[32,60,256]{2,0,1:T(8,128)(2,1)}, u32[]{:S(2)}, u32[]{:S(2)}) collective-permute-start(bf16[32,60,256]{2,0,1:T(8,128)(2,1)} %get-tuple-element.43), channel_id=1, source_target_pairs={{0,2},{2,4},{4,6},{6,8},{8,10},{10,12},{12,14},{14,16},{16,18},{18... | collective-permute-start | bytes 2949128 | tf_op jit(solution)/shard_map/ppermute | solution.py:12
  130.6 3.0 %fusion.166 = f32[256,1024]{1,0:T(8,128)} fusion(bf16[3584,256]{1,0:T(8,128)(2,1)S(1)} %fusion.159, bf16[3584,1024]{1,0:T(8,128)(2,1)S(1)} %fusion.6), kind=kOutput, calls=%fused_computation.304 | convolution fusion | flops 1879048192 | bytes 10223616 | tf_op jit(solution)/shard_map/dot_general | solution.py:100
  133.6 2.8 %stack.127 = f32[31,256]{1,0:T(8,128)S(1)} concatenate(f32[1,256]{1,0:T(1,128)} %bitcast.188, f32[1,256]{1,0:T(1,128)} %bitcast.187, f32[1,256]{1,0:T(1,128)} %bitcast.186, f32[1,256]{1,0:T(1,128)} %bitcast.185, f32[1,256]{1,0:T(1,128)} %bitcast.184, f32[1,256]{1,0:T(1,128)} %bitcast.183, f32[1,256]{1,0:T(1,128)} %bitcast.182, f32[1,256]{1,0:T(1,128)} %bitcast.181, ...), dimensions={0} | concatenate | bytes 63488 | tf_op jit(solution)/shard_map/stack | solution.py:88
  136.5 56.0 %psum.21 = f32[31,256]{1,0:T(8,128)S(1)} all-reduce(f32[31,256]{1,0:T(8,128)S(1)} %stack.127), channel_id=1, replica_groups=mesh['lon'=16,'lat'=2] {'lon','lat'}, use_global_device_ids=true, to_apply=%region_35.0 | all-reduce | flops 7936 | bytes 63488 | tf_op jit(solution)/shard_map/psum | solution.py:106
  193.1 6.5 %fusion.7 = bf16[3584,256]{1,0:T(8,128)(2,1)} fusion(bf16[3584,1024]{1,0:T(8,128)(2,1)} %copy-done.9, bf16[1024,256]{1,0:T(8,128)(2,1)} %param.9, bf16[3584,256]{1,0:T(8,128)(2,1)S(1)} %bitcast.93), kind=kOutput, calls=%fused_computation.67 | convolution fusion | flops 1881800704 | bytes 11534336 | tf_op jit(solution)/shard_map/dot_general | solution.py:54
  199.6 1.9 copy.12
  202.1 22.8 %fusion.73 = bf16[32,112,256]{2,1,0:T(8,128)(2,1)} fusion(f32[32,112,256]{2,1,0:T(8,128)S(1)} %bitcast.92, f32[32,60,256]{2,1,0:T(8,128)S(1)} %copy.12, f32[32,60,256]{2,1,0:T(8,128)S(1)} %copy.11, bf16[32,112,256]{2,1,0:T(8,128)(2,1)} %param.6, f32[256]{0:T(256)S(1)} %bitcast.117, f32[256]{0:T(256)S(1)} %bitcast.119, f32[256]{0:T(256)S(1)} %bitcast.123, ...), kind=kLoop, calls=%fused_computation.193 | loop fusion | flops 86245376 | bytes 11303936 | tf_op jit(solution)/shard_map/convert_element_type | solution.py:87
  224.9 45.9 %all-reduce.3.cloned.1.call-done = (f32[256,1024]{1,0:T(8,128)}, f32[1024,256]{1,0:T(8,128)}) async-done(((f32[256,1024]{1,0:T(8,128)}, f32[1024,256]{1,0:T(8,128)}), (f32[256,1024]{1,0:T(8,128)}, f32[1024,256]{1,0:T(8,128)})) %all-reduce.3.cloned.1.call-update) | async-done | bytes 2097168 | tf_op jit(solution)/shard_map/psum | solution.py:106
  270.8 2.3 broadcast_multiply_fusion.1
  273.2 2.3 broadcast_multiply_fusion
  (43 shorter events, 6.2 us)
Async XLA Ops:
  7.2 50.5 %copy-start = (bf16[256,1024]{1,0:T(8,128)(2,1)S(1)}, bf16[256,1024]{1,0:T(8,128)(2,1)}, u32[]{:S(2)}) copy-start(bf16[256,1024]{1,0:T(8,128)(2,1)} %param.8) | copy-start | bytes 1572868
  7.2 27.0 %copy-start.8 = (bf16[32,112,256]{2,1,0:T(8,128)(2,1)S(1)}, bf16[32,112,256]{2,1,0:T(8,128)(2,1)}, u32[]{:S(2)}) copy-start(bf16[32,112,256]{2,1,0:T(8,128)(2,1)} %param.5) | copy-start | bytes 5505028
  7.2 263.6 %all-reduce.3.cloned.1.call-start = ((), (), s32[]{:S(2)}) async-start(), calls=%async_computation | async-start | bytes 4194304 | tf_op jit(solution)/shard_map/psum | solution.py:106
  7.2 26.7 %collective-permute-start = (bf16[32,112,256]{2,1,0:T(8,128)(2,1)}, bf16[32,112,256]{2,1,0:T(8,128)(2,1)S(1)}, u32[]{:S(2)}, u32[]{:S(2)}) collective-permute-start(bf16[32,112,256]{2,1,0:T(8,128)(2,1)} %param.5), channel_id=1, source_target_pairs={{0,2},{2,4},{4,6},{6,8},{8,10},{10,12},{12,14},{14,16},{16,18},{18... | collective-permute-start | bytes 5505032 | tf_op jit(solution)/shard_map/ppermute | solution.py:12
  7.7 26.8 %collective-permute-start.1 = (bf16[32,112,256]{2,1,0:T(8,128)(2,1)}, bf16[32,112,256]{2,1,0:T(8,128)(2,1)S(1)}, u32[]{:S(2)}, u32[]{:S(2)}) collective-permute-start(bf16[32,112,256]{2,1,0:T(8,128)(2,1)} %param.5), channel_id=1, source_target_pairs={{0,30},{2,0},{4,2},{6,4},{8,6},{10,8},{12,10},{14,12},{16,14},{18,... | collective-permute-start | bytes 5505032 | tf_op jit(solution)/shard_map/ppermute | solution.py:12
  34.5 16.9 %copy-start.3 = (bf16[32,224,256]{2,1,0:T(8,128)(2,1)}, bf16[32,224,256]{2,1,0:T(8,128)(2,1)S(1)}, u32[]{:S(2)}) copy-start(bf16[32,224,256]{2,1,0:T(8,128)(2,1)S(1)} %get-tuple-element.44) | copy-start | bytes 11010052
  34.7 16.6 %copy-start.1 = (bf16[32,224,256]{2,1,0:T(8,128)(2,1)}, bf16[32,224,256]{2,1,0:T(8,128)(2,1)S(1)}, u32[]{:S(2)}) copy-start(bf16[32,224,256]{2,1,0:T(8,128)(2,1)S(1)} %constant_dynamic-update-slice_fusion.2) | copy-start | bytes 11010052
  57.7 7.9 %copy-start.11 = (bf16[1024,256]{1,0:T(8,128)(2,1)S(1)}, bf16[1024,256]{1,0:T(8,128)(2,1)}, u32[]{:S(2)}) copy-start(bf16[1024,256]{1,0:T(8,128)(2,1)} %param.9) | copy-start | bytes 1572868
  65.6 42.0 %copy-start.9 = (bf16[3584,1024]{1,0:T(8,128)(2,1)}, bf16[3584,1024]{1,0:T(8,128)(2,1)S(1)}, u32[]{:S(2)}) copy-start(bf16[3584,1024]{1,0:T(8,128)(2,1)S(1)} %get-tuple-element.77) | copy-start | bytes 22020100
  65.6 15.9 %copy-start.7 = (f32[32,112,256]{2,1,0:T(8,128)S(1)}, f32[32,112,256]{2,1,0:T(8,128)}, u32[]{:S(2)}) copy-start(f32[32,112,256]{2,1,0:T(8,128)} %get-tuple-element.41) | copy-start | bytes 11010052
  84.0 2.7 copy-start.4
  86.7 19.0 %copy-start.5 = (f32[3584,256]{1,0:T(8,128)}, f32[3584,256]{1,0:T(8,128)S(1)}, u32[]{:S(2)}) copy-start(f32[3584,256]{1,0:T(8,128)S(1)} %subtract_multiply_fusion) | copy-start | bytes 11010052
  86.7 9.4 %copy-start.2 = (bf16[32,224,256]{2,1,0:T(8,128)(2,1)S(1)}, bf16[32,224,256]{2,1,0:T(8,128)(2,1)}, u32[]{:S(2)}) copy-start(bf16[32,224,256]{2,1,0:T(8,128)(2,1)} %copy-done.1) | copy-start | bytes 11010052
  105.7 2.0 copy-start.10
  112.2 89.3 %collective-permute-start.2 = (bf16[32,60,256]{2,0,1:T(8,128)(2,1)}, bf16[32,60,256]{2,0,1:T(8,128)(2,1)S(1)}, u32[]{:S(2)}, u32[]{:S(2)}) collective-permute-start(bf16[32,60,256]{2,0,1:T(8,128)(2,1)} %get-tuple-element.42), channel_id=1, source_target_pairs={{0,30},{2,0},{4,2},{6,4},{8,6},{10,8},{12,10},{14,12},{16,14},{18,... | collective-permute-start | bytes 2949128 | tf_op jit(solution)/shard_map/ppermute | solution.py:12
  116.1 83.5 %collective-permute-start.3 = (bf16[32,60,256]{2,0,1:T(8,128)(2,1)}, bf16[32,60,256]{2,0,1:T(8,128)(2,1)}, u32[]{:S(2)}, u32[]{:S(2)}) collective-permute-start(bf16[32,60,256]{2,0,1:T(8,128)(2,1)} %get-tuple-element.43), channel_id=1, source_target_pairs={{0,2},{2,4},{4,6},{6,8},{8,10},{10,12},{12,14},{14,16},{16,18},{18... | collective-permute-start | bytes 2949128 | tf_op jit(solution)/shard_map/ppermute | solution.py:12
  199.6 2.5 copy-start.6
Sparse Core Ops, SparseCore 0:
  133.7 137.0 all-reduce.2
where the time goes:
time: 283 us; the launch traced here: 282 us
  other arithmetic  72.4 us (26%)
  waiting for transfers between devices  65.1 us (23%)
  blocking collectives  56 us (20%)
  matrix products  38.9 us (14%)
  starting transfers between devices  23.9 us (8%)
  between operations  14.3 us (5%)
  local copies, waits for them, and re-layouts  11.7 us (4%)
    psum x1, blocking collectives, per_device(): summed = lax.psum((kernel_terms, grad_up, grad_down), ('lon', 'lat'))  56 us
    psum x1, waiting for transfers between devices, per_device(): summed = lax.psum((kernel_terms, grad_up, grad_down), ('lon', 'lat'))  45.9 us
    ppermute x4, starting transfers between devices, passed_along(): lax.ppermute(value, axis, [(i, (i + by) % count) for i in range(count)])  23.9 us
    convert_element_type x1, other arithmetic, per_device(): (cotangent.astype(jnp.float32) + conv_back).astype(jnp.bfloat16)  22.8 us
    ppermute x4, waiting for transfers between devices, passed_along(): lax.ppermute(value, axis, [(i, (i + by) % count) for i in range(count)])  19.2 us
    reduce_sum x2, other arithmetic, per_device(): jnp.sum(wrapped_input[:, KERNEL_SPACING * index_of_tap:KERNEL_SPACING * i...  18.9 us
    reduce_sum x1, other arithmetic, per_device(): center = jnp.mean(conv, axis=-1, keepdims=True)  16.6 us
    dot_general x1, matrix products, per_device(): lax.dot_general(flat_cot, down_weight, contract_last, preferred_element_t...  15.9 us
  transfers between devices with their start and end apart: 5, of which 2 were waited for; matrix products, arithmetic and copies ran while one was open for 14% of the time, Pallas kernels for 0%

commit v1 on v0

--- a/solution.py
+++ b/solution.py
@@ -103,7 +103,8 @@
     grad_down = lax.dot_general(
         activated_low, flat_cot, contract_first, preferred_element_type=jnp.float32
     )
-    summed = lax.psum((kernel_terms, grad_up, grad_down), ("lon", "lat"))
+    _convert_stages_all = lambda body: lax.psum(lax.psum(body, axis_name="lat"), axis_name="lon")
+    summed = _convert_stages_all((kernel_terms, grad_up, grad_down))
     factor = 1.0 / math.sqrt(rows * column_list * lax.axis_size("lon") * lax.axis_size("lat"))
     return (output, field_grad, summed[0] * factor, summed[1] * factor, summed[2] * factor)
 

time: 283 us -> 341 us (1.20)
  other arithmetic: 72.4 us -> 109 us
  blocking collectives: 56 us -> 68.9 us
  local copies, waits for them, and re-layouts: 11.7 us -> 16.5 us
    convert_element_type x1, other arithmetic: 22.8 us -> 47 us  [per_device(): (cotangent.astype(jnp.float32) + conv_back).astype(jnp.bfloat16)]
    psum x1 -> x2, blocking collectives: 56 us -> 68.9 us  [the longest x1 59.8 us: per_device(): lax.psum(lax.psum(body, axis_name='lat'), axis_name='lon')]
    reduce_sum x2, other arithmetic: 18.9 us -> 28.4 us  [per_device(): jnp.sum(wrapped_input[:, KERNEL_SPACING * index_of_tap:KERNEL_SPACING * i...]
    psum x1 -> x2, waiting for transfers between devices: 45.9 us -> 47.3 us  [the longest x1 47.3 us: per_device(): lax.psum(lax.psum(body, axis_name='lat'), axis_name='lon')]
  transfers between devices with their start and end apart: 5 -> 6, of which waited for: 2 -> 2; matrix products, arithmetic and copies ran while one was open for 14% -> 24% of each run, Pallas kernels for 0% -> 0%
where the time goes in v1:
time: 341 us; the launch traced here: 340 us
  other arithmetic  109 us (32%)
  blocking collectives  68.9 us (20%)
  waiting for transfers between devices  66.5 us (20%)
  matrix products  41.2 us (12%)
  starting transfers between devices  24 us (7%)
  local copies, waits for them, and re-layouts  16.5 us (5%)
  between operations  14.2 us (4%)
    psum x1, blocking collectives, per_device(): lax.psum(lax.psum(body, axis_name='lat'), axis_name='lon')  59.8 us
    psum x1, waiting for transfers between devices, per_device(): lax.psum(lax.psum(body, axis_name='lat'), axis_name='lon')  47.3 us
    convert_element_type x1, other arithmetic, per_device(): (cotangent.astype(jnp.float32) + conv_back).astype(jnp.bfloat16)  47 us
    reduce_sum x2, other arithmetic, per_device(): jnp.sum(wrapped_input[:, KERNEL_SPACING * index_of_tap:KERNEL_SPACING * i...  28.4 us
    ppermute x4, starting transfers between devices, passed_along(): lax.ppermute(value, axis, [(i, (i + by) % count) for i in range(count)])  23.9 us
    ppermute x4, waiting for transfers between devices, passed_along(): lax.ppermute(value, axis, [(i, (i + by) % count) for i in range(count)])  19.2 us
    reduce_sum x1, other arithmetic, per_device(): center = jnp.mean(conv, axis=-1, keepdims=True)  16.6 us
    dot_general x1, matrix products, per_device(): lax.dot_general(flat_cot, down_weight, contract_last, preferred_element_t...  15.3 us
  transfers between devices with their start and end apart: 6, of which 2 were waited for; matrix products, arithmetic and copies ran while one was open for 24% of the time, Pallas kernels for 0%

profile of v1, /device:TPU:0, one launch (start us, length us, event | category | flops | bytes accessed | tf_op | source)
XLA Modules:
  0.0 340.2 jit_solution(14359421557109993822)
XLA Ops:
  7.7 5.0 %collective-permute-start.1 = (bf16[32,112,256]{2,1,0:T(8,128)(2,1)}, bf16[32,112,256]{2,1,0:T(8,128)(2,1)S(1)}, u32[]{:S(2)}, u32[]{:S(2)}) collective-permute-start(bf16[32,112,256]{2,1,0:T(8,128)(2,1)} %param.5), channel_id=1, source_target_pairs={{0,30},{2,0},{4,2},{6,4},{8,6},{10,8},{12,10},{14,12},{16,14},{18,... | collective-permute-start | bytes 5505032 | tf_op jit(solution)/shard_map/ppermute | solution.py:12
  14.8 19.2 %collective-permute-done = bf16[32,112,256]{2,1,0:T(8,128)(2,1)S(1)} collective-permute-done((bf16[32,112,256]{2,1,0:T(8,128)(2,1)}, bf16[32,112,256]{2,1,0:T(8,128)(2,1)S(1)}, u32[]{:S(2)}, u32[]{:S(2)}) %collective-permute-start) | collective-permute-done | bytes 1835040 | tf_op jit(solution)/shard_map/ppermute | solution.py:12
  34.8 16.6 %fusion.161 = (f32[32,112]{1,0:T(8,128)S(1)}, f32[32,112,256]{2,1,0:T(8,128)}) fusion(bf16[32,224,256]{2,1,0:T(8,128)(2,1)S(1)} %constant_dynamic-update-slice_fusion.2, f32[256]{0:T(256)S(1)} %bitcast.116, f32[256]{0:T(256)S(1)} %bitcast.118, f32[256]{0:T(256)S(1)} %bitcast.122, f32[256]{0:T(256)S(1)} %bitcast.124, f32[256]{0:T(256)S(1)} %bitcast.126, ...), kind=kLoop, calls=%fused_computation.300 | loop fusion | flops 85324288 | bytes 60601344 | tf_op jit(solution)/shard_map/reduce_sum | solution.py:41
  51.4 2.7 multiply_reduce_fusion.2
  54.3 3.4 %fusion.159 = bf16[3584,256]{1,0:T(8,128)(2,1)S(1)} fusion(f32[32,112,256]{2,1,0:T(8,128)} %get-tuple-element.43, f32[3584]{0:T(1024)S(1)} %rsqrt.12, f32[3584]{0:T(1024)S(1)} %div.15), kind=kLoop, calls=%fused_computation.287 | loop fusion | flops 2752512 | bytes 5533696 | tf_op jit(solution)/shard_map/convert_element_type | solution.py:46
  57.7 7.9 %multiply_convert_fusion = (bf16[3584,1024]{1,0:T(8,128)(2,1)S(1)}, f32[3584,1024]{1,0:T(8,128)}) fusion(bf16[3584,256]{1,0:T(8,128)(2,1)S(1)} %fusion.159, bf16[256,1024]{1,0:T(8,128)(2,1)S(1)} %copy-done), kind=kOutput, calls=%fused_computation.65 | convolution fusion | flops 1912078336 | bytes 24379392 | tf_op jit(solution)/shard_map/dot_general | solution.py:47
  65.6 15.3 %fusion.6 = bf16[3584,1024]{1,0:T(8,128)(2,1)S(1)} fusion(f32[3584,1024]{1,0:T(8,128)} %get-tuple-element.80, bf16[3584,256]{1,0:T(8,128)(2,1)S(1)} %bitcast.94, bf16[1024,256]{1,0:T(8,128)(2,1)S(1)} %copy-done.9), kind=kOutput, calls=%fused_computation.64 | convolution fusion | flops 1952448512 | bytes 24379392 | tf_op jit(solution)/shard_map/dot_general | solution.py:59
  81.0 3.0 fusion.166
  84.0 5.5 %fusion.160 = (f32[3584]{0:T(1024)S(1)}, f32[3584]{0:T(1024)S(1)}, f32[3584,256]{1,0:T(8,128)}) fusion(f32[3584]{0:T(1024)S(1)} %rsqrt.12, f32[3584]{0:T(1024)S(1)} %div.15, f32[32,112,256]{2,1,0:T(8,128)S(1)} %copy-done.5, bf16[3584,1024]{1,0:T(8,128)(2,1)S(1)} %fusion.6, bf16[256,1024]{1,0:T(8,128)(2,1)S(1)} %copy-done), kind=kOutput, calls=%fused_computation.299 | convolution fusion | flops 1883628544 | bytes 15261696 | tf_op jit(solution)/shard_map/dot_general | solution.py:63
  89.5 5.4 %subtract_multiply_fusion = f32[3584,256]{1,0:T(8,128)S(1)} fusion(f32[3584,256]{1,0:T(8,128)} %get-tuple-element.81, f32[32,112,256]{2,1,0:T(8,128)S(1)} %copy-done.5, f32[3584]{0:T(1024)S(1)} %get-tuple-element.82, f32[3584]{0:T(1024)S(1)} %get-tuple-element.83, f32[3584]{0:T(1024)S(1)} %rsqrt.12, f32[3584]{0:T(1024)S(1)} %div.15), kind=kLoop, calls=%fused_computation.284 | loop fusion | flops 5505024 | bytes 11067392 | tf_op jit(solution)/shard_map/mul | solution.py:68
  94.9 9.6 %fusion.67 = (f32[256]{0:T(256)S(1)}, f32[256]{0:T(256)S(1)}, f32[256]{0:T(256)S(1)}, f32[256]{0:T(256)S(1)}, f32[256]{0:T(256)S(1)}, /*index=5*/f32[256]{0:T(25...) fusion(f32[32,112,256]{2,1,0:T(8,128)S(1)} %bitcast.89, ...), kind=kLoop, calls=%fused_computation.187 | loop fusion | flops 44036096 | bytes 33046528 | tf_op jit(solution)/shard_map/reduce_sum | solution.py:90
  104.4 3.2 copy.14
  107.6 3.1 fusion.167
  110.7 2.6 fusion.163
  113.3 3.9 %collective-permute-start.2 = (bf16[32,60,256]{2,0,1:T(8,128)(2,1)}, bf16[32,60,256]{2,0,1:T(8,128)(2,1)}, u32[]{:S(2)}, u32[]{:S(2)}) collective-permute-start(bf16[32,60,256]{2,0,1:T(8,128)(2,1)} %get-tuple-element.44), channel_id=1, source_target_pairs={{0,30},{2,0},{4,2},{6,4},{8,6},{10,8},{12,10},{14,12},{16,14},{18,... | collective-permute-start | bytes 2949128 | tf_op jit(solution)/shard_map/ppermute | solution.py:12
  117.2 14.4 %collective-permute-start.3 = (bf16[32,60,256]{2,0,1:T(8,128)(2,1)S(1)}, bf16[32,60,256]{2,0,1:T(8,128)(2,1)}, u32[]{:S(2)}, u32[]{:S(2)}) collective-permute-start(bf16[32,60,256]{2,0,1:T(8,128)(2,1)S(1)} %get-tuple-element.45), channel_id=1, source_target_pairs={{0,2},{2,4},{4,6},{6,8},{8,10},{10,12},{12,14},{14,16},{16,18},{18... | collective-permute-start | bytes 2949128 | tf_op jit(solution)/shard_map/ppermute | solution.py:12
  131.7 18.9 %fusion.47 = (f32[256]{0:T(256)}, f32[256]{0:T(256)}, f32[256]{0:T(256)}, f32[256]{0:T(256)}, f32[256]{0:T(256)}, /*index=5*/f32[256]{0:T(256)}, f32[256]{0:T(25...) fusion(f32[32,112,256]{2,1,0:T(8,128)} %bitcast.91, ...), kind=kLoop, calls=%fused_computation.167 | loop fusion | flops 41283840 | bytes 31210496 | tf_op jit(solution)/shard_map/reduce_sum | solution.py:90
  150.6 2.9 stack.127
  153.5 9.1 %psum.42 = f32[31,256]{1,0:T(8,128)S(1)} all-reduce(f32[31,256]{1,0:T(8,128)S(1)} %stack.127), channel_id=1, replica_groups=mesh['lon'=16,'lat'=2] {'lat'}, use_global_device_ids=true, to_apply=%region_35.0 | all-reduce | flops 7936 | bytes 63488 | tf_op jit(solution)/shard_map/psum | solution.py:106
  162.6 59.8 %psum.43 = f32[31,256]{1,0:T(8,128)S(1)} all-reduce(f32[31,256]{1,0:T(8,128)S(1)} %psum.42), channel_id=1, replica_groups=mesh['lon'=16,'lat'=2] {'lon'}, use_global_device_ids=true, to_apply=%region_36.0 | all-reduce | flops 7936 | bytes 63488 | tf_op jit(solution)/shard_map/psum | solution.py:106
  223.0 6.4 %fusion.7 = bf16[3584,256]{1,0:T(8,128)(2,1)} fusion(bf16[3584,1024]{1,0:T(8,128)(2,1)} %copy-done.7, bf16[1024,256]{1,0:T(8,128)(2,1)} %param.9, bf16[3584,256]{1,0:T(8,128)(2,1)S(1)} %bitcast.93), kind=kOutput, calls=%fused_computation.67 | convolution fusion | flops 1881800704 | bytes 11534336 | tf_op jit(solution)/shard_map/dot_general | solution.py:54
  231.2 3.1 copy.11
  234.4 47.0 %fusion.73 = bf16[32,112,256]{2,1,0:T(8,128)(2,1)} fusion(f32[32,112,256]{2,1,0:T(8,128)} %bitcast.92, f32[32,60,256]{2,1,0:T(8,128)S(1)} %copy.12, f32[32,60,256]{2,1,0:T(8,128)} %copy.11, bf16[32,112,256]{2,1,0:T(8,128)(2,1)} %param.6, f32[256]{0:T(256)S(1)} %bitcast.117, f32[256]{0:T(256)S(1)} %bitcast.119, f32[256]{0:T(256)S(1)} %bitcast.123, ...), kind=kLoop, calls=%fused_computation.193 | loop fusion | flops 86245376 | bytes 11303936 | tf_op jit(solution)/shard_map/convert_element_type | solution.py:87
  281.4 47.3 %all-reduce.5.cloned.1.call-done = (f32[256,1024]{1,0:T(8,128)}, f32[1024,256]{1,0:T(8,128)}) async-done(((f32[256,1024]{1,0:T(8,128)}, f32[1024,256]{1,0:T(8,128)}), (f32[256,1024]{1,0:T(8,128)}, f32[1024,256]{1,0:T(8,128)})) %all-reduce.5.cloned.1.call-update) | async-done | bytes 2097168 | tf_op jit(solution)/shard_map/psum | solution.py:106
  (43 shorter events, 10.6 us)
Async XLA Ops:
  7.2 50.5 %copy-start = (bf16[256,1024]{1,0:T(8,128)(2,1)S(1)}, bf16[256,1024]{1,0:T(8,128)(2,1)}, u32[]{:S(2)}) copy-start(bf16[256,1024]{1,0:T(8,128)(2,1)} %param.8) | copy-start | bytes 1572868
  7.2 27.0 %copy-start.6 = (bf16[32,112,256]{2,1,0:T(8,128)(2,1)S(1)}, bf16[32,112,256]{2,1,0:T(8,128)(2,1)}, u32[]{:S(2)}) copy-start(bf16[32,112,256]{2,1,0:T(8,128)(2,1)} %param.5) | copy-start | bytes 5505028
  7.2 227.2 %all-reduce.7.cloned.1.call-start = ((), (), s32[]{:S(2)}) async-start(), calls=%async_computation.1 | async-start | bytes 4194304 | tf_op jit(solution)/shard_map/psum | solution.py:106
  7.2 26.7 %collective-permute-start = (bf16[32,112,256]{2,1,0:T(8,128)(2,1)}, bf16[32,112,256]{2,1,0:T(8,128)(2,1)S(1)}, u32[]{:S(2)}, u32[]{:S(2)}) collective-permute-start(bf16[32,112,256]{2,1,0:T(8,128)(2,1)} %param.5), channel_id=1, source_target_pairs={{0,2},{2,4},{4,6},{6,8},{8,10},{10,12},{12,14},{14,16},{16,18},{18... | collective-permute-start | bytes 5505032 | tf_op jit(solution)/shard_map/ppermute | solution.py:12
  7.7 26.8 %collective-permute-start.1 = (bf16[32,112,256]{2,1,0:T(8,128)(2,1)}, bf16[32,112,256]{2,1,0:T(8,128)(2,1)S(1)}, u32[]{:S(2)}, u32[]{:S(2)}) collective-permute-start(bf16[32,112,256]{2,1,0:T(8,128)(2,1)} %param.5), channel_id=1, source_target_pairs={{0,30},{2,0},{4,2},{6,4},{8,6},{10,8},{12,10},{14,12},{16,14},{18,... | collective-permute-start | bytes 5505032 | tf_op jit(solution)/shard_map/ppermute | solution.py:12
  34.5 16.9 %copy-start.3 = (bf16[32,224,256]{2,1,0:T(8,128)(2,1)}, bf16[32,224,256]{2,1,0:T(8,128)(2,1)S(1)}, u32[]{:S(2)}) copy-start(bf16[32,224,256]{2,1,0:T(8,128)(2,1)S(1)} %get-tuple-element.46) | copy-start | bytes 11010052
  34.7 16.6 %copy-start.1 = (bf16[32,224,256]{2,1,0:T(8,128)(2,1)}, bf16[32,224,256]{2,1,0:T(8,128)(2,1)S(1)}, u32[]{:S(2)}) copy-start(bf16[32,224,256]{2,1,0:T(8,128)(2,1)S(1)} %constant_dynamic-update-slice_fusion.2) | copy-start | bytes 11010052
  57.7 7.9 %copy-start.8 = (bf16[32,112,256]{2,1,0:T(8,128)(2,1)S(1)}, bf16[32,112,256]{2,1,0:T(8,128)(2,1)}, u32[]{:S(2)}) copy-start(bf16[32,112,256]{2,1,0:T(8,128)(2,1)} %param.6) | copy-start | bytes 5505028
  57.7 7.9 %copy-start.9 = (bf16[1024,256]{1,0:T(8,128)(2,1)S(1)}, bf16[1024,256]{1,0:T(8,128)(2,1)}, u32[]{:S(2)}) copy-start(bf16[1024,256]{1,0:T(8,128)(2,1)} %param.9) | copy-start | bytes 1572868
  65.6 42.0 %copy-start.7 = (bf16[3584,1024]{1,0:T(8,128)(2,1)}, bf16[3584,1024]{1,0:T(8,128)(2,1)S(1)}, u32[]{:S(2)}) copy-start(bf16[3584,1024]{1,0:T(8,128)(2,1)S(1)} %get-tuple-element.79) | copy-start | bytes 22020100
  80.9 3.1 copy-start.5
  89.5 5.4 %copy-start.2 = (bf16[32,224,256]{2,1,0:T(8,128)(2,1)S(1)}, bf16[32,224,256]{2,1,0:T(8,128)(2,1)}, u32[]{:S(2)}) copy-start(bf16[32,224,256]{2,1,0:T(8,128)(2,1)} %copy-done.1) | copy-start | bytes 11010052
  94.9 9.6 %copy-start.4 = (f32[3584,256]{1,0:T(8,128)}, f32[3584,256]{1,0:T(8,128)S(1)}, u32[]{:S(2)}) copy-start(f32[3584,256]{1,0:T(8,128)S(1)} %subtract_multiply_fusion) | copy-start | bytes 11010052
  113.3 118.0 %collective-permute-start.2 = (bf16[32,60,256]{2,0,1:T(8,128)(2,1)}, bf16[32,60,256]{2,0,1:T(8,128)(2,1)}, u32[]{:S(2)}, u32[]{:S(2)}) collective-permute-start(bf16[32,60,256]{2,0,1:T(8,128)(2,1)} %get-tuple-element.44), channel_id=1, source_target_pairs={{0,30},{2,0},{4,2},{6,4},{8,6},{10,8},{12,10},{14,12},{16,14},{18,... | collective-permute-start | bytes 2949128 | tf_op jit(solution)/shard_map/ppermute | solution.py:12
  117.2 112.2 %collective-permute-start.3 = (bf16[32,60,256]{2,0,1:T(8,128)(2,1)S(1)}, bf16[32,60,256]{2,0,1:T(8,128)(2,1)}, u32[]{:S(2)}, u32[]{:S(2)}) collective-permute-start(bf16[32,60,256]{2,0,1:T(8,128)(2,1)S(1)} %get-tuple-element.45), channel_id=1, source_target_pairs={{0,2},{2,4},{4,6},{6,8},{8,10},{10,12},{12,14},{14,16},{16,18},{18... | collective-permute-start | bytes 2949128 | tf_op jit(solution)/shard_map/ppermute | solution.py:12
  131.7 197.0 %all-reduce.5.cloned.1.call-start = ((), (), s32[]{:S(2)}) async-start(), calls=%async_computation | async-start | bytes 4194304 | tf_op jit(solution)/shard_map/psum | solution.py:106
Sparse Core Ops, SparseCore 0:
  131.8 64.6 all-reduce.6
  234.5 94.1 all-reduce.4
